TPU v7x, 256 devices: a whole 4x4x8 slice. The times are simulated.
256 devices in a mesh: seq: 64 (over x, z, core), head: 4 (over y).
Axes of the slice: x: 4, y: 4, z: 8, core: 2. Of those that a mesh axis runs over, the one named last changes fastest.
Arguments:
- queries: bfloat16 [16384, 64, 128], P(('seq', 'head')), may hold values from -64 to 64
- key_vectors: bfloat16 [16384, 64, 128], P(('seq', 'head')), may hold values from -5 to 5
- value_vectors: bfloat16 [16384, 64, 128], P(('seq', 'head')), may hold values from -6 to 6
- key_blocks: int32 [128, 12], P('seq'), may hold values from -1 to 125, as said below
Outputs:
- attended: bfloat16 [16384, 64, 128], P(('seq', 'head'))
Inputs may be any that keep to these rules, and one draw needn't show every extreme that they name: `key_blocks`: entries 2j and 2j+1 of row b are -1 or distinct blocks c with c // 2 == b // 2 - 2**j, never b - 1.
All inputs are finite; a program needn't handle non-finite values.
Results may differ from a plain program's by a relative error of at most 0.004.
Values may be sent and summed in bfloat16 or wider, within the bound.
A program may use at most 192 MiB of HBM per device.

v0:
```python
import math

import jax
import jax.numpy as jnp
from jax import lax
from jax.sharding import PartitionSpec as P

BLOCK = 128
LEVELS = 6


def from_behind(value, axis, by):
    size = lax.axis_size(axis)
    pairs = [(i, i + by) for i in range(size) if 0 <= i + by < size]
    return lax.ppermute(value, axis, pairs)


def absorb(carried, scores, apply_values):
    running_max, running_sum, weighted = carried
    new_max = jnp.maximum(running_max, jnp.max(scores, axis=-1))
    factor = jnp.exp(running_max - new_max)
    weights = jnp.exp(scores - new_max[..., None])
    running_sum = running_sum * factor + jnp.sum(weights, axis=-1)
    weighted = weighted * jnp.transpose(factor, (0, 2, 1))[..., None] + apply_values(
        weights.astype(jnp.bfloat16)
    )
    return (new_max, running_sum, weighted)


def local(queries, key_vectors, value_vectors, key_blocks):
    query_local, key_local, value_local = (
        lax.all_to_all(queries, "head", split_axis=1, concat_axis=0, tiled=True),
        lax.all_to_all(key_vectors, "head", split_axis=1, concat_axis=0, tiled=True),
        lax.all_to_all(value_vectors, "head", split_axis=1, concat_axis=0, tiled=True),
    )
    local_rows, head_count, head_width = query_local.shape
    blocks = local_rows // BLOCK
    device = lax.axis_index("seq")
    inverse_root = 1.0 / math.sqrt(head_width)
    query_tiles = query_local.reshape(blocks, BLOCK, head_count, head_width)
    query_ids = device * blocks + jnp.arange(blocks, dtype=jnp.int32)
    causal = jnp.arange(BLOCK)[:, None] >= jnp.arange(BLOCK)[None, :]
    carried = (
        jnp.full((blocks, head_count, BLOCK), -1e30, jnp.float32),
        jnp.zeros((blocks, head_count, BLOCK), jnp.float32),
        jnp.zeros((blocks, BLOCK, head_count, head_width), jnp.float32),
    )

    def dense_set(carried, near_keys, near_values, key_ids, with_diagonal):
        key_count = key_ids.shape[0]
        scores = (
            jnp.einsum("bqhd,nhd->bhqn", query_tiles, near_keys, preferred_element_type=jnp.float32)
            * inverse_root
        )
        scores = scores.reshape(blocks, head_count, BLOCK, key_count, BLOCK)
        listed = jnp.any(key_blocks[:, :, None] == key_ids[None, None, :], axis=1)
        window = key_ids[None, :] == query_ids[:, None] - 1
        allowed = (listed | window) & (key_ids >= 0)[None, :]
        allowed = allowed[:, None, None, :, None]
        if with_diagonal:
            diagonal = key_ids[None, :] == query_ids[:, None]
            allowed = allowed | diagonal[:, None, None, :, None] & causal[None, None, :, None, :]
        scores = jnp.where(allowed, scores, jnp.float32(-1e30)).reshape(
            blocks, head_count, BLOCK, key_count * BLOCK
        )

        def apply_values(rounded):
            return jnp.einsum(
                "bhqn,nhd->bqhd", rounded, near_values, preferred_element_type=jnp.float32
            )

        return absorb(carried, scores, apply_values)

    carried = dense_set(carried, key_local, value_local, query_ids, True)
    far_keys = key_local
    far_values = value_local
    for section in range(LEVELS):
        distance = 2**section
        far_keys, far_values = from_behind((key_local, value_local), "seq", distance)
        partner_ids = (device - distance) * blocks + jnp.arange(blocks, dtype=jnp.int32)
        carried = dense_set(carried, far_keys, far_values, partner_ids, False)
    running_max, running_sum, weighted = carried
    result = weighted / jnp.transpose(running_sum, (0, 2, 1))[..., None]
    result = result.astype(jnp.bfloat16).reshape(local_rows, head_count, head_width)
    return lax.all_to_all(result, "head", split_axis=0, concat_axis=1, tiled=True)


def solution(mesh):
    return jax.shard_map(
        local,
        mesh=mesh,
        in_specs=(
            P(("seq", "head"), None, None),
            P(("seq", "head"), None, None),
            P(("seq", "head"), None, None),
            P("seq", None),
        ),
        out_specs=P(("seq", "head"), None, None),
        check_vma=False,
    )
```

profile of v0, /device:TPU:5, one launch (start us, length us, event | category | flops | bytes accessed | tf_op | source)
XLA Modules:
  0.0 330.0 jit_solution(6914553099251389992)
XLA Ops:
  0.0 3.0 copy.31
  3.0 4.2 %all-to-all-start = ((bf16[64,64,128]{2,0,1:T(8,128)(2,1)}), bf16[64,64,128]{2,0,1:T(8,128)(2,1)S(1)}, u32[]{:S(2)}, u32[]{:S(2)}) async-start(bf16[64,64,128]{2,0,1:T(8,128)(2,1)} %copy.31), calls=%async_computation | async-start | bytes 2097152 | tf_op jit(solution)/shard_map/all_to_all | solution.py:33
  9.6 11.8 %all-to-all-done = bf16[64,64,128]{2,0,1:T(8,128)(2,1)S(1)} async-done(((bf16[64,64,128]{2,0,1:T(8,128)(2,1)}), bf16[64,64,128]{2,0,1:T(8,128)(2,1)S(1)}, u32[]{:S(2)}, u32[]{:S(2)}) %all-to-all-start) | async-done | bytes 1048608 | tf_op jit(solution)/shard_map/all_to_all | solution.py:33
  21.4 3.5 %all-to-all-start.1 = ((bf16[64,64,128]{2,0,1:T(8,128)(2,1)}), bf16[64,64,128]{2,0,1:T(8,128)(2,1)S(1)}, u32[]{:S(2)}, u32[]{:S(2)}) async-start(bf16[64,64,128]{2,0,1:T(8,128)(2,1)} %copy.33), calls=%async_computation.1 | async-start | bytes 2097152 | tf_op jit(solution)/shard_map/all_to_all | solution.py:32
  25.0 2.9 copy.35
  28.3 2.8 collective-permute-start.8
  31.1 7.2 %all-to-all-done.1 = bf16[64,64,128]{2,0,1:T(8,128)(2,1)S(1)} async-done(((bf16[64,64,128]{2,0,1:T(8,128)(2,1)}), bf16[64,64,128]{2,0,1:T(8,128)(2,1)S(1)}, u32[]{:S(2)}, u32[]{:S(2)}) %all-to-all-start.1) | async-done | bytes 1048608 | tf_op jit(solution)/shard_map/all_to_all | solution.py:32
  38.3 4.2 %all-to-all-start.2 = ((bf16[64,64,128]{2,0,1:T(8,128)(2,1)}), bf16[64,64,128]{2,0,1:T(8,128)(2,1)}, u32[]{:S(2)}, u32[]{:S(2)}) async-start(bf16[64,64,128]{2,0,1:T(8,128)(2,1)} %copy.35), calls=%async_computation.2 | async-start | bytes 2097152 | tf_op jit(solution)/shard_map/all_to_all | solution.py:34
  42.7 8.8 %collective-permute-start.6 = (bf16[256,16,128]{2,0,1:T(8,128)(2,1)S(1)}, bf16[256,16,128]{2,0,1:T(8,128)(2,1)}, u32[]{:S(2)}, u32[]{:S(2)}) collective-permute-start(bf16[256,16,128]{2,0,1:T(8,128)(2,1)S(1)} %bitcast.383), channel_id=1, source_target_pairs={{0,32},{4,36},{8,40},{12,44},{16,48},{20,52},{24,56},{28,60},{32,6... | collective-permute-start | bytes 3145736 | tf_op jit(solution)/shard_map/ppermute | solution.py:15
  51.9 3.1 collective-permute-start.4
  55.0 2.6 collective-permute-start.2
  57.6 5.0 %collective-permute-start = (bf16[256,16,128]{2,0,1:T(8,128)(2,1)S(1)}, bf16[256,16,128]{2,0,1:T(8,128)(2,1)}, u32[]{:S(2)}, u32[]{:S(2)}) collective-permute-start(bf16[256,16,128]{2,0,1:T(8,128)(2,1)S(1)} %bitcast.386), channel_id=1, source_target_pairs={{0,4},{4,8},{8,12},{12,16},{16,20},{20,24},{24,28},{28,32},{32,36}... | collective-permute-start | bytes 3145736 | tf_op jit(solution)/shard_map/ppermute | solution.py:15
  66.2 2.0 fusion.19
  68.2 9.2 %collective-permute-done.6 = bf16[256,16,128]{2,0,1:T(8,128)(2,1)} collective-permute-done((bf16[256,16,128]{2,0,1:T(8,128)(2,1)S(1)}, bf16[256,16,128]{2,0,1:T(8,128)(2,1)}, u32[]{:S(2)}, u32[]{:S(2)}) %collective-permute-start.6) | collective-permute-done | bytes 1048608 | tf_op jit(solution)/shard_map/ppermute | solution.py:15
  77.4 17.7 %collective-permute-start.1 = (bf16[256,16,128]{2,0,1:T(8,128)(2,1)S(1)}, bf16[256,16,128]{2,0,1:T(8,128)(2,1)S(1)}, u32[]{:S(2)}, u32[]{:S(2)}) collective-permute-start(bf16[256,16,128]{2,0,1:T(8,128)(2,1)S(1)} %bitcast.375), channel_id=1, source_target_pairs={{0,4},{4,8},{8,12},{12,16},{16,20},{20,24},{24,28},{28,32},{32,36}... | collective-permute-start | bytes 3145736 | tf_op jit(solution)/shard_map/ppermute | solution.py:15
  95.1 2.0 fusion.18
  97.1 29.7 %collective-permute-done.4 = bf16[256,16,128]{2,0,1:T(8,128)(2,1)} collective-permute-done((bf16[256,16,128]{2,0,1:T(8,128)(2,1)S(1)}, bf16[256,16,128]{2,0,1:T(8,128)(2,1)}, u32[]{:S(2)}, u32[]{:S(2)}) %collective-permute-start.4) | collective-permute-done | bytes 1048608 | tf_op jit(solution)/shard_map/ppermute | solution.py:15
  126.9 19.0 %collective-permute-start.3 = (bf16[256,16,128]{2,0,1:T(8,128)(2,1)S(1)}, bf16[256,16,128]{2,0,1:T(8,128)(2,1)S(1)}, u32[]{:S(2)}, u32[]{:S(2)}) collective-permute-start(bf16[256,16,128]{2,0,1:T(8,128)(2,1)S(1)} %bitcast.376), channel_id=1, source_target_pairs={{0,8},{4,12},{8,16},{12,20},{16,24},{20,28},{24,32},{28,36},{32,40... | collective-permute-start | bytes 3145736 | tf_op jit(solution)/shard_map/ppermute | solution.py:15
  145.9 2.0 fusion.17
  147.9 17.4 %collective-permute-done.2 = bf16[256,16,128]{2,0,1:T(8,128)(2,1)} collective-permute-done((bf16[256,16,128]{2,0,1:T(8,128)(2,1)S(1)}, bf16[256,16,128]{2,0,1:T(8,128)(2,1)}, u32[]{:S(2)}, u32[]{:S(2)}) %collective-permute-start.2) | collective-permute-done | bytes 1048608 | tf_op jit(solution)/shard_map/ppermute | solution.py:15
  165.2 4.3 %collective-permute-start.5 = (bf16[256,16,128]{2,0,1:T(8,128)(2,1)S(1)}, bf16[256,16,128]{2,0,1:T(8,128)(2,1)S(1)}, u32[]{:S(2)}, u32[]{:S(2)}) collective-permute-start(bf16[256,16,128]{2,0,1:T(8,128)(2,1)S(1)} %bitcast.377), channel_id=1, source_target_pairs={{0,16},{4,20},{8,24},{12,28},{16,32},{20,36},{24,40},{28,44},{32,4... | collective-permute-start | bytes 3145736 | tf_op jit(solution)/shard_map/ppermute | solution.py:15
  169.5 2.0 fusion.16
  171.5 12.3 %collective-permute-done = bf16[256,16,128]{2,0,1:T(8,128)(2,1)} collective-permute-done((bf16[256,16,128]{2,0,1:T(8,128)(2,1)S(1)}, bf16[256,16,128]{2,0,1:T(8,128)(2,1)}, u32[]{:S(2)}, u32[]{:S(2)}) %collective-permute-start) | collective-permute-done | bytes 1048608 | tf_op jit(solution)/shard_map/ppermute | solution.py:15
  183.8 2.2 collective-permute-start.7
  186.0 2.0 fusion.15
  188.1 2.1 collective-permute-start.9
  195.1 20.7 %collective-permute-done.1 = bf16[256,16,128]{2,0,1:T(8,128)(2,1)S(1)} collective-permute-done((bf16[256,16,128]{2,0,1:T(8,128)(2,1)S(1)}, bf16[256,16,128]{2,0,1:T(8,128)(2,1)S(1)}, u32[]{:S(2)}, u32[]{:S(2)}) %collective-permute-start.1) | collective-permute-done | bytes 1048608 | tf_op jit(solution)/shard_map/ppermute | solution.py:15
  219.4 37.0 %collective-permute-done.3 = bf16[256,16,128]{2,0,1:T(8,128)(2,1)S(1)} collective-permute-done((bf16[256,16,128]{2,0,1:T(8,128)(2,1)S(1)}, bf16[256,16,128]{2,0,1:T(8,128)(2,1)S(1)}, u32[]{:S(2)}, u32[]{:S(2)}) %collective-permute-start.3) | collective-permute-done | bytes 1048608 | tf_op jit(solution)/shard_map/ppermute | solution.py:15
  258.7 8.4 %collective-permute-done.5 = bf16[256,16,128]{2,0,1:T(8,128)(2,1)S(1)} collective-permute-done((bf16[256,16,128]{2,0,1:T(8,128)(2,1)S(1)}, bf16[256,16,128]{2,0,1:T(8,128)(2,1)S(1)}, u32[]{:S(2)}, u32[]{:S(2)}) %collective-permute-start.5) | collective-permute-done | bytes 1048608 | tf_op jit(solution)/shard_map/ppermute | solution.py:15
  269.4 29.9 %collective-permute-done.7 = bf16[256,16,128]{2,0,1:T(8,128)(2,1)S(1)} collective-permute-done((bf16[256,16,128]{2,0,1:T(8,128)(2,1)S(1)}, bf16[256,16,128]{2,0,1:T(8,128)(2,1)S(1)}, u32[]{:S(2)}, u32[]{:S(2)}) %collective-permute-start.7) | collective-permute-done | bytes 1048608 | tf_op jit(solution)/shard_map/ppermute | solution.py:15
  303.3 5.9 %fusion.36 = bf16[2,128,16,128]{3,1,0,2:T(8,128)(2,1)S(1)} fusion(f32[16,2,128,128]{3,2,1,0:T(8,128)S(1)} %fusion.23, f32[16,2,128,128]{3,2,1,0:T(8,128)S(1)} %fusion.25, f32[16,2,128,128]{3,2,1,0:T(8,128)S(1)} %fusion.27, f32[16,2,128,128]{3,2,1,0:T(8,128)S(1)} %fusion.29, f32[16,2,128,128]{3,2,1,0:T(8,128)S(1)} %fusion.31, ...), kind=kOutput, calls=%fused_computation.44 | convolution fusion | flops 280494080 | bytes 19022336 | tf_op jit(solution)/shard_map/bhqn,nhd->bqhd/dot_general | solution.py:68
  309.9 18.8 %all_to_all.69 = bf16[256,16,128]{2,1,0:T(8,128)(2,1)S(1)} all-to-all(bf16[256,16,128]{2,1,0:T(8,128)(2,1)S(1)} %copy.44), channel_id=1, replica_groups=mesh['seq'=64,'head'=4] {'head'}, dimensions={0} | all-to-all | bytes 2097152 | tf_op jit(solution)/shard_map/all_to_all | solution.py:85
  (65 shorter events, 25.6 us)
Async XLA Ops:
  0.0 7.3 %copy-start = (bf16[64,64,128]{2,1,0:T(8,128)(2,1)S(1)}, bf16[64,64,128]{2,1,0:T(8,128)(2,1)}, u32[]{:S(2)}) copy-start(bf16[64,64,128]{2,1,0:T(8,128)(2,1)} %param.4) | copy-start | bytes 3145732
  0.0 8.9 %copy-start.1 = (s32[2,12]{1,0:T(2,128)S(1)}, s32[2,12]{1,0:T(2,128)}, u32[]{:S(2)}) copy-start(s32[2,12]{1,0:T(2,128)} %param.7) | copy-start | bytes 292
  3.0 18.4 %all-to-all-start = ((bf16[64,64,128]{2,0,1:T(8,128)(2,1)}), bf16[64,64,128]{2,0,1:T(8,128)(2,1)S(1)}, u32[]{:S(2)}, u32[]{:S(2)}) async-start(bf16[64,64,128]{2,0,1:T(8,128)(2,1)} %copy.31), calls=%async_computation | async-start | bytes 2097152 | tf_op jit(solution)/shard_map/all_to_all | solution.py:33
  21.4 16.9 %all-to-all-start.1 = ((bf16[64,64,128]{2,0,1:T(8,128)(2,1)}), bf16[64,64,128]{2,0,1:T(8,128)(2,1)S(1)}, u32[]{:S(2)}, u32[]{:S(2)}) async-start(bf16[64,64,128]{2,0,1:T(8,128)(2,1)} %copy.33), calls=%async_computation.1 | async-start | bytes 2097152 | tf_op jit(solution)/shard_map/all_to_all | solution.py:32
  28.3 36.6 %collective-permute-start.8 = (bf16[256,16,128]{2,0,1:T(8,128)(2,1)S(1)}, bf16[256,16,128]{2,0,1:T(8,128)(2,1)}, u32[]{:S(2)}, u32[]{:S(2)}) collective-permute-start(bf16[256,16,128]{2,0,1:T(8,128)(2,1)S(1)} %bitcast.382), channel_id=1, source_target_pairs={{0,64},{4,68},{8,72},{12,76},{16,80},{20,84},{24,88},{28,92},{32,9... | collective-permute-start | bytes 3145736 | tf_op jit(solution)/shard_map/ppermute | solution.py:15
  38.3 24.5 %all-to-all-start.2 = ((bf16[64,64,128]{2,0,1:T(8,128)(2,1)}), bf16[64,64,128]{2,0,1:T(8,128)(2,1)}, u32[]{:S(2)}, u32[]{:S(2)}) async-start(bf16[64,64,128]{2,0,1:T(8,128)(2,1)} %copy.35), calls=%async_computation.2 | async-start | bytes 2097152 | tf_op jit(solution)/shard_map/all_to_all | solution.py:34
  42.7 34.7 %collective-permute-start.6 = (bf16[256,16,128]{2,0,1:T(8,128)(2,1)S(1)}, bf16[256,16,128]{2,0,1:T(8,128)(2,1)}, u32[]{:S(2)}, u32[]{:S(2)}) collective-permute-start(bf16[256,16,128]{2,0,1:T(8,128)(2,1)S(1)} %bitcast.383), channel_id=1, source_target_pairs={{0,32},{4,36},{8,40},{12,44},{16,48},{20,52},{24,56},{28,60},{32,6... | collective-permute-start | bytes 3145736 | tf_op jit(solution)/shard_map/ppermute | solution.py:15
  51.9 75.0 %collective-permute-start.4 = (bf16[256,16,128]{2,0,1:T(8,128)(2,1)S(1)}, bf16[256,16,128]{2,0,1:T(8,128)(2,1)}, u32[]{:S(2)}, u32[]{:S(2)}) collective-permute-start(bf16[256,16,128]{2,0,1:T(8,128)(2,1)S(1)} %bitcast.384), channel_id=1, source_target_pairs={{0,16},{4,20},{8,24},{12,28},{16,32},{20,36},{24,40},{28,44},{32,4... | collective-permute-start | bytes 3145736 | tf_op jit(solution)/shard_map/ppermute | solution.py:15
  55.0 110.3 %collective-permute-start.2 = (bf16[256,16,128]{2,0,1:T(8,128)(2,1)S(1)}, bf16[256,16,128]{2,0,1:T(8,128)(2,1)}, u32[]{:S(2)}, u32[]{:S(2)}) collective-permute-start(bf16[256,16,128]{2,0,1:T(8,128)(2,1)S(1)} %bitcast.385), channel_id=1, source_target_pairs={{0,8},{4,12},{8,16},{12,20},{16,24},{20,28},{24,32},{28,36},{32,40... | collective-permute-start | bytes 3145736 | tf_op jit(solution)/shard_map/ppermute | solution.py:15
  57.6 126.2 %collective-permute-start = (bf16[256,16,128]{2,0,1:T(8,128)(2,1)S(1)}, bf16[256,16,128]{2,0,1:T(8,128)(2,1)}, u32[]{:S(2)}, u32[]{:S(2)}) collective-permute-start(bf16[256,16,128]{2,0,1:T(8,128)(2,1)S(1)} %bitcast.386), channel_id=1, source_target_pairs={{0,4},{4,8},{8,12},{12,16},{16,20},{20,24},{24,28},{28,32},{32,36}... | collective-permute-start | bytes 3145736 | tf_op jit(solution)/shard_map/ppermute | solution.py:15
  64.9 123.2 %collective-permute-start.10 = (bf16[256,16,128]{2,0,1:T(8,128)(2,1)S(1)}, bf16[256,16,128]{2,0,1:T(8,128)(2,1)S(1)}, u32[]{:S(2)}, u32[]{:S(2)}) collective-permute-start(bf16[256,16,128]{2,0,1:T(8,128)(2,1)S(1)} %bitcast.388), channel_id=1, source_target_pairs={{0,128},{4,132},{8,136},{12,140},{16,144},{20,148},{24,152},{28,15... | collective-permute-start | bytes 3145736 | tf_op jit(solution)/shard_map/ppermute | solution.py:15
  77.4 138.4 %collective-permute-start.1 = (bf16[256,16,128]{2,0,1:T(8,128)(2,1)S(1)}, bf16[256,16,128]{2,0,1:T(8,128)(2,1)S(1)}, u32[]{:S(2)}, u32[]{:S(2)}) collective-permute-start(bf16[256,16,128]{2,0,1:T(8,128)(2,1)S(1)} %bitcast.375), channel_id=1, source_target_pairs={{0,4},{4,8},{8,12},{12,16},{16,20},{20,24},{24,28},{28,32},{32,36}... | collective-permute-start | bytes 3145736 | tf_op jit(solution)/shard_map/ppermute | solution.py:15
  126.9 129.5 %collective-permute-start.3 = (bf16[256,16,128]{2,0,1:T(8,128)(2,1)S(1)}, bf16[256,16,128]{2,0,1:T(8,128)(2,1)S(1)}, u32[]{:S(2)}, u32[]{:S(2)}) collective-permute-start(bf16[256,16,128]{2,0,1:T(8,128)(2,1)S(1)} %bitcast.376), channel_id=1, source_target_pairs={{0,8},{4,12},{8,16},{12,20},{16,24},{20,28},{24,32},{28,36},{32,40... | collective-permute-start | bytes 3145736 | tf_op jit(solution)/shard_map/ppermute | solution.py:15
  165.2 101.9 %collective-permute-start.5 = (bf16[256,16,128]{2,0,1:T(8,128)(2,1)S(1)}, bf16[256,16,128]{2,0,1:T(8,128)(2,1)S(1)}, u32[]{:S(2)}, u32[]{:S(2)}) collective-permute-start(bf16[256,16,128]{2,0,1:T(8,128)(2,1)S(1)} %bitcast.377), channel_id=1, source_target_pairs={{0,16},{4,20},{8,24},{12,28},{16,32},{20,36},{24,40},{28,44},{32,4... | collective-permute-start | bytes 3145736 | tf_op jit(solution)/shard_map/ppermute | solution.py:15
  183.8 115.6 %collective-permute-start.7 = (bf16[256,16,128]{2,0,1:T(8,128)(2,1)S(1)}, bf16[256,16,128]{2,0,1:T(8,128)(2,1)S(1)}, u32[]{:S(2)}, u32[]{:S(2)}) collective-permute-start(bf16[256,16,128]{2,0,1:T(8,128)(2,1)S(1)} %bitcast.378), channel_id=1, source_target_pairs={{0,32},{4,36},{8,40},{12,44},{16,48},{20,52},{24,56},{28,60},{32,6... | collective-permute-start | bytes 3145736 | tf_op jit(solution)/shard_map/ppermute | solution.py:15
  188.1 112.7 %collective-permute-start.9 = (bf16[256,16,128]{2,0,1:T(8,128)(2,1)S(1)}, bf16[256,16,128]{2,0,1:T(8,128)(2,1)S(1)}, u32[]{:S(2)}, u32[]{:S(2)}) collective-permute-start(bf16[256,16,128]{2,0,1:T(8,128)(2,1)S(1)} %bitcast.379), channel_id=1, source_target_pairs={{0,64},{4,68},{8,72},{12,76},{16,80},{20,84},{24,88},{28,92},{32,9... | collective-permute-start | bytes 3145736 | tf_op jit(solution)/shard_map/ppermute | solution.py:15
  215.8 87.4 %collective-permute-start.11 = (bf16[256,16,128]{2,0,1:T(8,128)(2,1)S(1)}, bf16[256,16,128]{2,0,1:T(8,128)(2,1)S(1)}, u32[]{:S(2)}, u32[]{:S(2)}) collective-permute-start(bf16[256,16,128]{2,0,1:T(8,128)(2,1)S(1)} %bitcast.380), channel_id=1, source_target_pairs={{0,128},{4,132},{8,136},{12,140},{16,144},{20,148},{24,152},{28,15... | collective-permute-start | bytes 3145736 | tf_op jit(solution)/shard_map/ppermute | solution.py:15
where the time goes:
time: 331 us; the launch traced here: 330 us
  waiting for transfers between devices  184 us (56%)
  starting transfers between devices  82.2 us (25%)
  matrix products  25.2 us (8%)
  blocking collectives  18.8 us (6%)
  local copies, waits for them, and re-layouts  11.7 us (4%)
  other arithmetic  8.07 us (2%)
    ppermute x12, waiting for transfers between devices, from_behind(): return lax.ppermute(value, axis, pairs)  165 us
    ppermute x12, starting transfers between devices, from_behind(): return lax.ppermute(value, axis, pairs)  70.3 us
    all_to_all x1, blocking collectives, local(): lax.all_to_all(result, 'head', split_axis=0, concat_axis=1, tiled=True)  18.8 us
    dot_general x7, matrix products, apply_values(): jnp.einsum('bhqn,nhd->bqhd', rounded, near_values, preferred_element_type...  13.5 us
    all_to_all x1, waiting for transfers between devices, local(): lax.all_to_all(key_vectors, 'head', split_axis=1, concat_axis=0, tiled=True)  11.8 us
    dot_general x7, matrix products, dense_set(): jnp.einsum('bqhd,nhd->bhqn', query_tiles, near_keys, preferred_element_ty...  11.7 us
    unnamed x23, local copies, waits for them, and re-layouts  8.21 us
    all_to_all x1, waiting for transfers between devices, local(): lax.all_to_all(queries, 'head', split_axis=1, concat_axis=0, tiled=True)  7.19 us
  transfers between devices with their start and end apart: 15, of which 10 were waited for; matrix products, arithmetic and copies ran while one was open for 10% of the time, Pallas kernels for 0%

commit v1 on v0

v1 whole, which is shorter than its diff:
```python
import math

import jax
import jax.numpy as jnp
from jax import lax
from jax.experimental import pallas as pl
from jax.experimental.pallas import tpu as pltpu
from jax.sharding import PartitionSpec as P

BLOCK = 128
LEVELS = 6
XS, ZS, CS, YS = 4, 8, 2, 4
PEERS = ZS * CS * YS
PAIRS = ZS * CS
PIECE = 64
NEG = -1e30
MESH = pl.DeviceIdType.MESH


def kernel(kb_ref, src_ref, out_ref, kv, qs, bias, own_bias, outs, scores, *sems):
    kv_send, kv_recv, q_send, q_recv, b_send, b_recv, x1_send, x1_recv, x2_send, x2_recv, o_send, o_recv = sems
    seq = lax.axis_index("seq")
    y = lax.axis_index("head")
    x = seq // (ZS * CS)
    pair = seq % PAIRS
    z = pair // CS
    core = pair % CS
    my_head = y * PAIRS + pair
    my_slot = pair * YS + y

    def device_of(x_, pair_, y_):
        return (x_ * PAIRS + pair_, y_)

    def offset(i):
        return i % ZS, (i // ZS) % CS, i // (ZS * CS)

    def toward(i):
        dz, dc, dy = offset(i)
        return ((z + dz) % ZS) * CS + (core + dc) % CS, (y + dy) % YS

    def behind(i):
        dz, dc, dy = offset(i)
        return ((z + ZS - dz) % ZS) * CS + (core + CS - dc) % CS, (y + YS - dy) % YS

    barrier = pltpu.get_barrier_semaphore()

    def greet(i, carry):
        pair_, y_ = toward(i)
        pl.semaphore_signal(barrier, inc=1, device_id=device_of(x, pair_, y_), device_id_type=MESH)
        return carry

    lax.fori_loop(1, PEERS, greet, 0)
    for step in (1, 2):
        @pl.when(x + step < XS)
        def _():
            pl.semaphore_signal(barrier, inc=1, device_id=device_of(x + step, pair, y), device_id_type=MESH)

        @pl.when(x >= step)
        def _():
            pl.semaphore_signal(barrier, inc=1, device_id=device_of(x - step, pair, y), device_id_type=MESH)

    for block in range(2):
        for level in range(LEVELS):
            for key in range(2):
                key_id = 2 * (seq - 2**level) + key
                hit = (kb_ref[block, 0] == key_id)
                for entry in range(1, 2 * LEVELS):
                    hit = hit | (kb_ref[block, entry] == key_id)
                hit = hit | (key_id == 2 * seq + block - 1)
                value = jnp.where(hit & (key_id >= 0), jnp.float32(0.0), jnp.float32(NEG))
                own_bias[block * 8 + level : block * 8 + level + 1, key * BLOCK : (key + 1) * BLOCK] = jnp.full(
                    (1, BLOCK), value, jnp.float32
                )

    @pl.when(x == 0)
    def _():
        kv[PEERS : 2 * PEERS] = jnp.zeros((PEERS, 2 * PIECE, 128), kv.dtype)

    @pl.when(x <= 1)
    def _():
        kv[0:PEERS] = jnp.zeros((PEERS, 2 * PIECE, 128), kv.dtype)

    near = 2 * PEERS

    own_kv = pltpu.make_async_copy(src_ref.at[my_head, pl.ds(0, 2 * PIECE)], kv.at[near + my_slot], kv_recv.at[0])
    own_q = pltpu.make_async_copy(src_ref.at[my_head, pl.ds(2 * PIECE, PIECE)], qs.at[my_slot], q_recv.at[0])
    own_kv.start()
    own_q.start()
    both = (x + 1 < XS).astype(jnp.int32) + (x + 2 < XS).astype(jnp.int32) + (x >= 1).astype(jnp.int32) + (x >= 2).astype(jnp.int32)
    pl.semaphore_wait(barrier, PEERS - 1 + both)

    def send_kv(i, carry):
        pair_, y_ = toward(i)
        pltpu.make_async_remote_copy(
            src_ref.at[y_ * PAIRS + pair_, pl.ds(0, 2 * PIECE)],
            kv.at[near + my_slot],
            kv_send.at[0],
            kv_recv.at[i],
            device_id=device_of(x, pair_, y_),
            device_id_type=MESH,
        ).start()
        return carry

    def send_q(i, carry):
        pair_, y_ = toward(i)
        pltpu.make_async_remote_copy(
            src_ref.at[y_ * PAIRS + pair_, pl.ds(2 * PIECE, PIECE)],
            qs.at[my_slot],
            q_send.at[0],
            q_recv.at[0],
            device_id=device_of(x, pair_, y_),
            device_id_type=MESH,
        ).start()
        return carry

    def send_bias(i, carry):
        pair_, y_ = toward(i)
        pltpu.make_async_remote_copy(
            own_bias, bias.at[pair], b_send.at[0], b_recv.at[0], device_id=device_of(x, pair_, y_), device_id_type=MESH
        ).start()
        return carry

    lax.fori_loop(1, PEERS, send_kv, 0)
    lax.fori_loop(1, PEERS, send_q, 0)
    own_b = pltpu.make_async_copy(own_bias, bias.at[pair], b_recv.at[0])
    own_b.start()
    lax.fori_loop(1, PAIRS, send_bias, 0)

    def forward(i, carry):
        pair_, y_ = behind(i)
        slot = pair_ * YS + y_
        here = kv.at[near + slot]
        pltpu.make_async_copy(here, here, kv_recv.at[i]).wait()
        for step, send, recv in ((1, x1_send, x1_recv), (2, x2_send, x2_recv)):
            @pl.when(x + step < XS)
            def _():
                pltpu.make_async_remote_copy(
                    here,
                    kv.at[near - step * PEERS + slot],
                    send.at[0],
                    recv.at[0],
                    device_id=device_of(x + step, pair, y),
                    device_id_type=MESH,
                ).start()
        return carry

    lax.fori_loop(0, PEERS, forward, 0)
    for step, recv in ((1, x1_recv), (2, x2_recv)):
        @pl.when(x >= step)
        def _():
            whole = kv.at[pl.ds(near - step * PEERS, PEERS)]
            pltpu.make_async_copy(whole, whole, recv.at[0]).wait()

    pltpu.make_async_copy(bias, bias, b_recv.at[0]).wait()
    pltpu.make_async_copy(qs, qs, q_recv.at[0]).wait()

    scale = math.log2(math.e) / math.sqrt(128.0)

    def half(p, d, part):
        return kv[pl.ds(YS * (2 * PAIRS + p - d), YS), part * PIECE : (part + 1) * PIECE, :].reshape(2 * BLOCK, 128)

    def attend(p):
        q = qs[pl.ds(YS * p, YS)].reshape(2 * BLOCK, 128)
        peak = None
        for level in range(LEVELS + 1):
            d = 0 if level == LEVELS else 2**level
            s = lax.dot_general(q, half(p, d, 0), (((1,), (1,)), ((), ())), preferred_element_type=jnp.float32)
            if d == 0:
                row = lax.broadcasted_iota(jnp.int32, (2 * BLOCK, 2 * BLOCK), 0)
                col = lax.broadcasted_iota(jnp.int32, (2 * BLOCK, 2 * BLOCK), 1)
                s = jnp.where(col <= row, s, NEG)
                scores[level] = s
            else:
                s0 = s[0:BLOCK] + bias[p, level : level + 1, :]
                s1 = s[BLOCK:] + bias[p, 8 + level : 9 + level, :]
                s = jnp.concatenate([s0, s1], axis=0)
                scores[level] = s
            top = jnp.maximum(s[:, 0:BLOCK], s[:, BLOCK:])
            peak = top if peak is None else jnp.maximum(peak, top)
        peak = jnp.max(peak, axis=1, keepdims=True)
        total = None
        acc = None
        for level in range(LEVELS + 1):
            d = 0 if level == LEVELS else 2**level
            w = jnp.exp2((scores[level] - peak) * scale)
            part = w[:, 0:BLOCK] + w[:, BLOCK:]
            total = part if total is None else total + part
            o = jnp.dot(w.astype(jnp.bfloat16), half(p, d, 1), preferred_element_type=jnp.float32)
            acc = o if acc is None else acc + o
        norm = jnp.sum(total, axis=1, keepdims=True)
        outs[pl.ds(YS * p, YS)] = (acc / norm).astype(jnp.bfloat16).reshape(YS, PIECE, 128)

    def give_back(p):
        for y_ in range(YS):
            here = outs.at[YS * p + y_]
            there = out_ref.at[my_head]
            mine = (p == pair) & (y == y_)

            @pl.when(mine)
            def _():
                pltpu.make_async_copy(here, there, o_recv.at[0]).start()

            @pl.when(jnp.logical_not(mine))
            def _():
                pltpu.make_async_remote_copy(
                    here, there, o_send.at[0], o_recv.at[0], device_id=device_of(x, p, y_), device_id_type=MESH
                ).start()

    def step(k, carry):
        attend((pair + k) % PAIRS)

        @pl.when(k >= 1)
        def _():
            give_back((pair + k + PAIRS - 1) % PAIRS)

        return carry

    lax.fori_loop(0, PAIRS, step, 0)
    give_back((pair + PAIRS - 1) % PAIRS)

    most = kv.at[pl.ds(near, PEERS - 1)]
    pltpu.make_async_copy(most, most, kv_send.at[0]).wait()
    most = qs.at[pl.ds(0, PEERS - 1)]
    pltpu.make_async_copy(most, most, q_send.at[0]).wait()
    most = bias.at[pl.ds(0, PAIRS - 1)]
    pltpu.make_async_copy(most, most, b_send.at[0]).wait()
    for step_, send in ((1, x1_send), (2, x2_send)):
        @pl.when(x + step_ < XS)
        def _():
            whole = kv.at[pl.ds(near, PEERS)]
            pltpu.make_async_copy(whole, whole, send.at[0]).wait()
    most = outs.at[pl.ds(0, PEERS - 1)]
    pltpu.make_async_copy(most, most, o_send.at[0]).wait()
    pltpu.make_async_copy(out_ref, out_ref, o_recv.at[0]).wait()


def local(queries, key_vectors, value_vectors, key_blocks):
    rows = jnp.concatenate([key_vectors, value_vectors, queries], axis=0)
    by_head = jnp.transpose(rows, (1, 0, 2))
    dma = pltpu.SemaphoreType.DMA
    result = pl.pallas_call(
        kernel,
        out_shape=jax.ShapeDtypeStruct((PEERS, PIECE, 128), jnp.bfloat16),
        in_specs=[pl.BlockSpec(memory_space=pltpu.SMEM), pl.BlockSpec(memory_space=pltpu.VMEM)],
        out_specs=pl.BlockSpec(memory_space=pltpu.VMEM),
        scratch_shapes=[
            pltpu.VMEM((3 * PEERS, 2 * PIECE, 128), jnp.bfloat16),
            pltpu.VMEM((PEERS, PIECE, 128), jnp.bfloat16),
            pltpu.VMEM((PAIRS, 16, 2 * BLOCK), jnp.float32),
            pltpu.VMEM((16, 2 * BLOCK), jnp.float32),
            pltpu.VMEM((PEERS, PIECE, 128), jnp.bfloat16),
            pltpu.VMEM((LEVELS + 1, 2 * BLOCK, 2 * BLOCK), jnp.float32),
            dma((1,)), dma((PEERS,)),
            dma((1,)), dma((1,)),
            dma((1,)), dma((1,)),
            dma((1,)), dma((1,)),
            dma((1,)), dma((1,)),
            dma((1,)), dma((1,)),
        ],
        compiler_params=pltpu.CompilerParams(collective_id=0, has_side_effects=True, vmem_limit_bytes=48 * 2**20),
    )(key_blocks, by_head)
    return jnp.transpose(result, (1, 0, 2))


def solution(mesh):
    return jax.shard_map(
        local,
        mesh=mesh,
        in_specs=(
            P(("seq", "head"), None, None),
            P(("seq", "head"), None, None),
            P(("seq", "head"), None, None),
            P("seq", None),
        ),
        out_specs=P(("seq", "head"), None, None),
        check_vma=False,
    )
```

time: 331 us -> 150 us (0.45)
  waiting for transfers between devices: 184 us -> 0 us
  Pallas kernels: 0 us -> 143 us
  starting transfers between devices: 82.2 us -> 0 us
  matrix products: 25.2 us -> 0 us
  blocking collectives: 18.8 us -> 0 us
  other arithmetic: 8.07 us -> 0.28 us
  local copies, waits for them, and re-layouts: 11.7 us -> 6.62 us
    ppermute x12 -> x0, waiting for transfers between devices: 165 us -> none  [from_behind(): return lax.ppermute(value, axis, pairs)]
    pallas_call x0 -> x1, Pallas kernels: none -> 143 us  [local(): pl.pallas_call(kernel, out_shape=jax.ShapeDtypeStruct((PEERS, PIECE, 128)...]
    ppermute x12 -> x0, starting transfers between devices: 70.3 us -> none  [from_behind(): return lax.ppermute(value, axis, pairs)]
    dot_general x14 -> x0, matrix products: 25.2 us -> none  [the longest x7 13.5 us: apply_values(): jnp.einsum('bhqn,nhd->bqhd', rounded, near_values, preferred_element_type...]
    all_to_all x3 -> x0, waiting for transfers between devices: 19 us -> none  [the longest x1 11.8 us: local(): lax.all_to_all(key_vectors, 'head', split_axis=1, concat_axis=0, tiled=True)]
    all_to_all x1 -> x0, blocking collectives: 18.8 us -> none  [local(): lax.all_to_all(result, 'head', split_axis=0, concat_axis=1, tiled=True)]
    all_to_all x3 -> x0, starting transfers between devices: 12 us -> none  [the longest x1 4.25 us: local(): lax.all_to_all(value_vectors, 'head', split_axis=1, concat_axis=0, tiled=...]
    reduce_sum x7 -> x0, other arithmetic: 7.06 us -> none  [absorb(): running_sum = running_sum * factor + jnp.sum(weights, axis=-1)]
  transfers between devices with their start and end apart: 15 -> 0, of which waited for: 10 -> 0; matrix products, arithmetic and copies ran while one was open for 10% -> 0% of each run, Pallas kernels for 0% -> 0%
where the time goes in v1:
time: 150 us
  Pallas kernels  143 us (95%)
  local copies, waits for them, and re-layouts  6.62 us (4%)
    pallas_call x1, Pallas kernels, local(): pl.pallas_call(kernel, out_shape=jax.ShapeDtypeStruct((PEERS, PIECE, 128)...  143 us
    unnamed x7, local copies, waits for them, and re-layouts  4.97 us

profile of v1, /device:TPU:5, one launch (start us, length us, event | category | flops | bytes accessed | tf_op | source)
XLA Modules:
  0.0 149.6 jit_solution(10816034837689424261)
XLA Ops:
  0.0 0.0 copy-start.1
  0.0 2.0 %copy.7 = bf16[64,64,128]{2,0,1:T(8,128)(2,1)S(1)} copy(bf16[64,64,128]{2,1,0:T(8,128)(2,1)} %param.4) | data formatting | bytes 2097152 | tf_op args[0]
  2.0 1.9 %copy.5 = bf16[64,64,128]{2,0,1:T(8,128)(2,1)S(1)} copy(bf16[64,64,128]{2,1,0:T(8,128)(2,1)} %param.5) | data formatting | bytes 2097152 | tf_op args[1]
  3.9 0.0 copy-done.1
  3.9 0.7 copy.6
  4.6 0.0 copy-start
  4.6 0.3 maximum_bitcast_fusion.src_ref
  4.9 0.4 copy-done
  5.3 142.6 %shard_map.46 = bf16[64,64,128]{2,1,0:T(8,128)(2,1)S(1)} custom-call(s32[2,12]{1,0:T(2,128)S(1)} %copy-done, bf16[64,192,128]{2,1,0:T(8,128)(2,1)S(1)} %maximum_bitcast_fusion.src_ref), custom_call_target="tpu_custom_call" | custom-call | tf_op jit(solution)/shard_map/pallas_call | solution.py:241
  147.9 1.6 %copy.8 = bf16[64,64,128]{2,1,0:T(8,128)(2,1)} copy(bf16[64,64,128]{2,0,1:T(8,128)(2,1)S(1)} %bitcast.3) | data formatting | bytes 2097152 | tf_op jit(solution)/shard_map/transpose | solution.py:262
Async XLA Ops:
  0.0 3.9 %copy-start.1 = (bf16[64,64,128]{2,1,0:T(8,128)(2,1)S(1)}, bf16[64,64,128]{2,1,0:T(8,128)(2,1)}, u32[]{:S(2)}) copy-start(bf16[64,64,128]{2,1,0:T(8,128)(2,1)} %param.6) | copy-start | bytes 3145732
  4.6 0.7 copy-start

commit v2 on v1

--- a/solution.py
+++ b/solution.py
@@ -17,8 +17,15 @@
 MESH = pl.DeviceIdType.MESH
 
 
-def kernel(kb_ref, src_ref, out_ref, kv, qs, bias, own_bias, outs, scores, *sems):
-    kv_send, kv_recv, q_send, q_recv, b_send, b_recv, x1_send, x1_recv, x2_send, x2_recv, o_send, o_recv = sems
+RELAY = 3
+AHEAD = PEERS // RELAY + 1
+BACK = PEERS - AHEAD
+LAG = 8
+
+
+def kernel(kb_ref, src_ref, out_ref, kv, stage, qs, bias, own_bias, outs, scores, *sems):
+    kv_send, kv_recv, q_send, q_recv, b_send, b_recv = sems[:6]
+    up_send, upa_recv, upb_recv, down_send, down_recv, on_send, two_recv, o_send, o_recv = sems[6:]
     seq = lax.axis_index("seq")
     y = lax.axis_index("head")
     x = seq // (ZS * CS)
@@ -32,7 +39,8 @@
         return (x_ * PAIRS + pair_, y_)
 
     def offset(i):
-        return i % ZS, (i // ZS) % CS, i // (ZS * CS)
+        j = i // (CS * YS)
+        return ((j + 1) // 2) * (2 * (j % 2) - 1) + ZS, (i // YS) % CS, i % YS
 
     def toward(i):
         dz, dc, dy = offset(i)
@@ -40,7 +48,7 @@
 
     def behind(i):
         dz, dc, dy = offset(i)
-        return ((z + ZS - dz) % ZS) * CS + (core + CS - dc) % CS, (y + YS - dy) % YS
+        return ((z + 2 * ZS - dz) % ZS) * CS + (core + CS - dc) % CS, (y + YS - dy) % YS
 
     barrier = pltpu.get_barrier_semaphore()
 
@@ -50,14 +58,9 @@
         return carry
 
     lax.fori_loop(1, PEERS, greet, 0)
-    for step in (1, 2):
-        @pl.when(x + step < XS)
-        def _():
-            pl.semaphore_signal(barrier, inc=1, device_id=device_of(x + step, pair, y), device_id_type=MESH)
-
-        @pl.when(x >= step)
-        def _():
-            pl.semaphore_signal(barrier, inc=1, device_id=device_of(x - step, pair, y), device_id_type=MESH)
+    x_up, x_down = (x + 1) % XS, (x + XS - 1) % XS
+    for x_ in (x_up, x_down):
+        pl.semaphore_signal(barrier, inc=1, device_id=device_of(x_, pair, y), device_id_type=MESH)
 
     for block in range(2):
         for level in range(LEVELS):
@@ -83,11 +86,10 @@
     near = 2 * PEERS
 
     own_kv = pltpu.make_async_copy(src_ref.at[my_head, pl.ds(0, 2 * PIECE)], kv.at[near + my_slot], kv_recv.at[0])
-    own_q = pltpu.make_async_copy(src_ref.at[my_head, pl.ds(2 * PIECE, PIECE)], qs.at[my_slot], q_recv.at[0])
+    own_q = pltpu.make_async_copy(src_ref.at[my_head, pl.ds(2 * PIECE, PIECE)], qs.at[my_slot], q_recv.at[pair])
     own_kv.start()
     own_q.start()
-    both = (x + 1 < XS).astype(jnp.int32) + (x + 2 < XS).astype(jnp.int32) + (x >= 1).astype(jnp.int32) + (x >= 2).astype(jnp.int32)
-    pl.semaphore_wait(barrier, PEERS - 1 + both)
+    pl.semaphore_wait(barrier, PEERS - 1 + 2)
 
     def send_kv(i, carry):
         pair_, y_ = toward(i)
@@ -107,14 +109,14 @@
             src_ref.at[y_ * PAIRS + pair_, pl.ds(2 * PIECE, PIECE)],
             qs.at[my_slot],
             q_send.at[0],
-            q_recv.at[0],
+            q_recv.at[pair],
             device_id=device_of(x, pair_, y_),
             device_id_type=MESH,
         ).start()
         return carry
 
     def send_bias(i, carry):
-        pair_, y_ = toward(i)
+        pair_, y_ = toward(YS * i)
         pltpu.make_async_remote_copy(
             own_bias, bias.at[pair], b_send.at[0], b_recv.at[0], device_id=device_of(x, pair_, y_), device_id_type=MESH
         ).start()
@@ -126,33 +128,81 @@
     own_b.start()
     lax.fori_loop(1, PAIRS, send_bias, 0)
 
-    def forward(i, carry):
+    def arrived(piece, recv):
+        pltpu.make_async_copy(piece, piece, recv).wait()
+
+    def piece_of(i):
         pair_, y_ = behind(i)
-        slot = pair_ * YS + y_
+        return pair_ * YS + y_
+
+    def pass_on(source, target, send, recv, x_):
+        pltpu.make_async_remote_copy(
+            source, target, send, recv, device_id=device_of(x_, pair, y), device_id_type=MESH
+        ).start()
+
+    def forward(i):
+        slot = piece_of(i)
         here = kv.at[near + slot]
-        pltpu.make_async_copy(here, here, kv_recv.at[i]).wait()
-        for step, send, recv in ((1, x1_send, x1_recv), (2, x2_send, x2_recv)):
-            @pl.when(x + step < XS)
+        arrived(here, kv_recv.at[i])
+        ahead = i % RELAY == 0
+
+        @pl.when((x < XS - 1) & ahead)
+        def _():
+            pass_on(here, kv.at[near - PEERS + slot], up_send.at[0], upa_recv.at[i // RELAY], x_up)
+
+        @pl.when((x < XS - 1) & jnp.logical_not(ahead))
+        def _():
+            pass_on(here, kv.at[near - PEERS + slot], up_send.at[0], upb_recv.at[0], x_up)
+
+        @pl.when((x < 2) & jnp.logical_not(ahead))
+        def _():
+            pass_on(here, stage.at[slot], down_send.at[0], down_recv.at[i], x_down)
+
+    def relay(i):
+        slot = piece_of(i)
+        ahead = i % RELAY == 0
+
+        @pl.when((x >= 1) & ahead)
+        def _():
+            here = kv.at[near - PEERS + slot]
+            arrived(here, upa_recv.at[i // RELAY])
+
+            @pl.when(x < XS - 1)
             def _():
-                pltpu.make_async_remote_copy(
-                    here,
-                    kv.at[near - step * PEERS + slot],
-                    send.at[0],
-                    recv.at[0],
-                    device_id=device_of(x + step, pair, y),
-                    device_id_type=MESH,
-                ).start()
-        return carry
-
-    lax.fori_loop(0, PEERS, forward, 0)
-    for step, recv in ((1, x1_recv), (2, x2_recv)):
-        @pl.when(x >= step)
-        def _():
-            whole = kv.at[pl.ds(near - step * PEERS, PEERS)]
-            pltpu.make_async_copy(whole, whole, recv.at[0]).wait()
-
-    pltpu.make_async_copy(bias, bias, b_recv.at[0]).wait()
-    pltpu.make_async_copy(qs, qs, q_recv.at[0]).wait()
+                pass_on(here, kv.at[slot], on_send.at[0], two_recv.at[0], x_up)
+
+        @pl.when(((x == 0) | (x == XS - 1)) & jnp.logical_not(ahead))
+        def _():
+            here = stage.at[slot]
+            arrived(here, down_recv.at[i])
+            pass_on(here, kv.at[slot], on_send.at[0], two_recv.at[0], x_down)
+
+    def both_steps(i, carry):
+        forward(i)
+
+        @pl.when(i >= LAG)
+        def _():
+            relay(i - LAG)
+
+        return carry
+
+    lax.fori_loop(0, PEERS, both_steps, 0)
+
+    def last_steps(i, carry):
+        relay(i)
+        return carry
+
+    lax.fori_loop(PEERS - LAG, PEERS, last_steps, 0)
+
+    @pl.when(x >= 1)
+    def _():
+        arrived(kv.at[pl.ds(near - PEERS, BACK)], upb_recv.at[0])
+
+    @pl.when(x >= 2)
+    def _():
+        arrived(kv.at[pl.ds(0, PEERS)], two_recv.at[0])
+
+    arrived(bias, b_recv.at[0])
 
     scale = math.log2(math.e) / math.sqrt(128.0)
 
@@ -206,32 +256,45 @@
                     here, there, o_send.at[0], o_recv.at[0], device_id=device_of(x, p, y_), device_id_type=MESH
                 ).start()
 
+    def turn(k):
+        return toward(YS * k)[0]
+
     def step(k, carry):
-        attend((pair + k) % PAIRS)
+        p = turn(k)
+        arrived(qs.at[pl.ds(YS * p, YS)], q_recv.at[p])
+        attend(p)
 
         @pl.when(k >= 1)
         def _():
-            give_back((pair + k + PAIRS - 1) % PAIRS)
+            give_back(turn(k - 1))
 
         return carry
 
     lax.fori_loop(0, PAIRS, step, 0)
-    give_back((pair + PAIRS - 1) % PAIRS)
-
-    most = kv.at[pl.ds(near, PEERS - 1)]
-    pltpu.make_async_copy(most, most, kv_send.at[0]).wait()
-    most = qs.at[pl.ds(0, PEERS - 1)]
-    pltpu.make_async_copy(most, most, q_send.at[0]).wait()
-    most = bias.at[pl.ds(0, PAIRS - 1)]
-    pltpu.make_async_copy(most, most, b_send.at[0]).wait()
-    for step_, send in ((1, x1_send), (2, x2_send)):
-        @pl.when(x + step_ < XS)
-        def _():
-            whole = kv.at[pl.ds(near, PEERS)]
-            pltpu.make_async_copy(whole, whole, send.at[0]).wait()
-    most = outs.at[pl.ds(0, PEERS - 1)]
-    pltpu.make_async_copy(most, most, o_send.at[0]).wait()
-    pltpu.make_async_copy(out_ref, out_ref, o_recv.at[0]).wait()
+    give_back(turn(PAIRS - 1))
+
+    arrived(kv.at[pl.ds(near, PEERS - 1)], kv_send.at[0])
+    arrived(qs.at[pl.ds(0, PEERS - 1)], q_send.at[0])
+    arrived(bias.at[pl.ds(0, PAIRS - 1)], b_send.at[0])
+
+    @pl.when(x < XS - 1)
+    def _():
+        arrived(kv.at[pl.ds(near, PEERS)], up_send.at[0])
+
+    @pl.when(x < 2)
+    def _():
+        arrived(stage.at[pl.ds(0, BACK)], down_send.at[0])
+
+    @pl.when((x >= 1) & (x < XS - 1))
+    def _():
+        arrived(kv.at[pl.ds(0, AHEAD)], on_send.at[0])
+
+    @pl.when((x == 0) | (x == XS - 1))
+    def _():
+        arrived(kv.at[pl.ds(0, BACK)], on_send.at[0])
+
+    arrived(outs.at[pl.ds(0, PEERS - 1)], o_send.at[0])
+    arrived(out_ref, o_recv.at[0])
 
 
 def local(queries, key_vectors, value_vectors, key_blocks):
@@ -245,15 +308,17 @@
         out_specs=pl.BlockSpec(memory_space=pltpu.VMEM),
         scratch_shapes=[
             pltpu.VMEM((3 * PEERS, 2 * PIECE, 128), jnp.bfloat16),
+            pltpu.VMEM((PEERS, 2 * PIECE, 128), jnp.bfloat16),
             pltpu.VMEM((PEERS, PIECE, 128), jnp.bfloat16),
             pltpu.VMEM((PAIRS, 16, 2 * BLOCK), jnp.float32),
             pltpu.VMEM((16, 2 * BLOCK), jnp.float32),
             pltpu.VMEM((PEERS, PIECE, 128), jnp.bfloat16),
             pltpu.VMEM((LEVELS + 1, 2 * BLOCK, 2 * BLOCK), jnp.float32),
             dma((1,)), dma((PEERS,)),
+            dma((1,)), dma((PAIRS,)),
             dma((1,)), dma((1,)),
-            dma((1,)), dma((1,)),
-            dma((1,)), dma((1,)),
+            dma((1,)), dma((AHEAD,)), dma((1,)),
+            dma((1,)), dma((PEERS,)),
             dma((1,)), dma((1,)),
             dma((1,)), dma((1,)),
         ],

time: 150 us -> 132 us (0.88); the launches traced: 150 us -> 130 us
  Pallas kernels: 143 us -> 123 us
    pallas_call x1, Pallas kernels: 143 us -> 123 us  [local(): pl.pallas_call(kernel, out_shape=jax.ShapeDtypeStruct((PEERS, PIECE, 128)...]
where the time goes in v2:
time: 132 us; the launch traced here: 130 us
  Pallas kernels  123 us (93%)
  local copies, waits for them, and re-layouts  6.62 us (5%)
    pallas_call x1, Pallas kernels, local(): pl.pallas_call(kernel, out_shape=jax.ShapeDtypeStruct((PEERS, PIECE, 128)...  123 us
    unnamed x7, local copies, waits for them, and re-layouts  4.97 us

profile of v2, /device:TPU:5, one launch (start us, length us, event | category | flops | bytes accessed | tf_op | source)
XLA Modules:
  0.0 129.7 jit_solution(5716362743845269018)
XLA Ops:
  0.0 0.0 copy-start.1
  0.0 2.0 %copy.7 = bf16[64,64,128]{2,0,1:T(8,128)(2,1)S(1)} copy(bf16[64,64,128]{2,1,0:T(8,128)(2,1)} %param.4) | data formatting | bytes 2097152 | tf_op args[0]
  2.0 1.9 %copy.5 = bf16[64,64,128]{2,0,1:T(8,128)(2,1)S(1)} copy(bf16[64,64,128]{2,1,0:T(8,128)(2,1)} %param.5) | data formatting | bytes 2097152 | tf_op args[1]
  3.9 0.0 copy-done.1
  3.9 0.7 copy.6
  4.6 0.0 copy-start
  4.6 0.3 maximum_bitcast_fusion.src_ref
  4.9 0.4 copy-done
  5.3 122.8 %shard_map.46 = bf16[64,64,128]{2,1,0:T(8,128)(2,1)S(1)} custom-call(s32[2,12]{1,0:T(2,128)S(1)} %copy-done, bf16[64,192,128]{2,1,0:T(8,128)(2,1)S(1)} %maximum_bitcast_fusion.src_ref), custom_call_target="tpu_custom_call" | custom-call | tf_op jit(solution)/shard_map/pallas_call | solution.py:304
  128.1 1.6 %copy.8 = bf16[64,64,128]{2,1,0:T(8,128)(2,1)} copy(bf16[64,64,128]{2,0,1:T(8,128)(2,1)S(1)} %bitcast.3) | data formatting | bytes 2097152 | tf_op jit(solution)/shard_map/transpose | solution.py:327
Async XLA Ops:
  0.0 3.9 %copy-start.1 = (bf16[64,64,128]{2,1,0:T(8,128)(2,1)S(1)}, bf16[64,64,128]{2,1,0:T(8,128)(2,1)}, u32[]{:S(2)}) copy-start(bf16[64,64,128]{2,1,0:T(8,128)(2,1)} %param.6) | copy-start | bytes 3145732
  4.6 0.7 copy-start

commit v3 on v2

--- a/solution.py
+++ b/solution.py
@@ -20,6 +20,7 @@
 RELAY = 3
 AHEAD = PEERS // RELAY + 1
 BACK = PEERS - AHEAD
+WINDOW = 32
 LAG = 8
 
 
@@ -104,7 +105,7 @@
         return carry
 
     def send_q(i, carry):
-        pair_, y_ = toward(i)
+        pair_, y_ = toward(PEERS - i)
         pltpu.make_async_remote_copy(
             src_ref.at[y_ * PAIRS + pair_, pl.ds(2 * PIECE, PIECE)],
             qs.at[my_slot],
@@ -122,8 +123,7 @@
         ).start()
         return carry
 
-    lax.fori_loop(1, PEERS, send_kv, 0)
-    lax.fori_loop(1, PEERS, send_q, 0)
+    lax.fori_loop(1, WINDOW, send_kv, 0)
     own_b = pltpu.make_async_copy(own_bias, bias.at[pair], b_recv.at[0])
     own_b.start()
     lax.fori_loop(1, PAIRS, send_bias, 0)
@@ -179,6 +179,15 @@
 
     def both_steps(i, carry):
         forward(i)
+
+        @pl.when(i + WINDOW < PEERS)
+        def _():
+            send_kv(i + WINDOW, 0)
+
+        @pl.when(i + WINDOW >= PEERS)
+        def _():
+            first = 1 + 2 * (i + WINDOW - PEERS)
+            lax.fori_loop(first, jnp.minimum(first + 2, PEERS), send_q, 0)
 
         @pl.when(i >= LAG)
         def _():
@@ -257,7 +266,7 @@
                 ).start()
 
     def turn(k):
-        return toward(YS * k)[0]
+        return toward(YS * (PAIRS - 1 - k))[0]
 
     def step(k, carry):
         p = turn(k)

time: 132 us -> 120 us (0.909); the launches traced: 130 us -> 120 us
  Pallas kernels: 123 us -> 113 us
    pallas_call x1, Pallas kernels: 123 us -> 113 us  [local(): pl.pallas_call(kernel, out_shape=jax.ShapeDtypeStruct((PEERS, PIECE, 128)...]
where the time goes in v3:
time: 120 us
  Pallas kernels  113 us (94%)
  local copies, waits for them, and re-layouts  6.62 us (6%)
    pallas_call x1, Pallas kernels, local(): pl.pallas_call(kernel, out_shape=jax.ShapeDtypeStruct((PEERS, PIECE, 128)...  113 us
    unnamed x7, local copies, waits for them, and re-layouts  4.97 us

profile of v3, /device:TPU:5, one launch (start us, length us, event | category | flops | bytes accessed | tf_op | source)
XLA Modules:
  0.0 119.9 jit_solution(4959088867875186450)
XLA Ops:
  0.0 0.0 copy-start.1
  0.0 2.0 %copy.7 = bf16[64,64,128]{2,0,1:T(8,128)(2,1)S(1)} copy(bf16[64,64,128]{2,1,0:T(8,128)(2,1)} %param.4) | data formatting | bytes 2097152 | tf_op args[0]
  2.0 1.9 %copy.5 = bf16[64,64,128]{2,0,1:T(8,128)(2,1)S(1)} copy(bf16[64,64,128]{2,1,0:T(8,128)(2,1)} %param.5) | data formatting | bytes 2097152 | tf_op args[1]
  3.9 0.0 copy-done.1
  3.9 0.7 copy.6
  4.6 0.0 copy-start
  4.6 0.3 maximum_bitcast_fusion.src_ref
  4.9 0.4 copy-done
  5.3 113.0 %shard_map.46 = bf16[64,64,128]{2,1,0:T(8,128)(2,1)S(1)} custom-call(s32[2,12]{1,0:T(2,128)S(1)} %copy-done, bf16[64,192,128]{2,1,0:T(8,128)(2,1)S(1)} %maximum_bitcast_fusion.src_ref), custom_call_target="tpu_custom_call" | custom-call | tf_op jit(solution)/shard_map/pallas_call | solution.py:313
  118.3 1.6 %copy.8 = bf16[64,64,128]{2,1,0:T(8,128)(2,1)} copy(bf16[64,64,128]{2,0,1:T(8,128)(2,1)S(1)} %bitcast.3) | data formatting | bytes 2097152 | tf_op jit(solution)/shard_map/transpose | solution.py:336
Async XLA Ops:
  0.0 3.9 %copy-start.1 = (bf16[64,64,128]{2,1,0:T(8,128)(2,1)S(1)}, bf16[64,64,128]{2,1,0:T(8,128)(2,1)}, u32[]{:S(2)}) copy-start(bf16[64,64,128]{2,1,0:T(8,128)(2,1)} %param.6) | copy-start | bytes 3145732
  4.6 0.7 copy-start

commit v4 on v3

--- a/solution.py
+++ b/solution.py
@@ -24,9 +24,12 @@
 LAG = 8
 
 
-def kernel(kb_ref, src_ref, out_ref, kv, stage, qs, bias, own_bias, outs, scores, *sems):
-    kv_send, kv_recv, q_send, q_recv, b_send, b_recv = sems[:6]
-    up_send, upa_recv, upb_recv, down_send, down_recv, on_send, two_recv, o_send, o_recv = sems[6:]
+def kernel(kb_ref, k_ref, v_ref, q_ref, out_ref, raw, src_ref, kv, stage, qs, bias, own_bias, outs, scores, *sems):
+    in_sem, kv_send, kv_recv, q_send, q_recv, b_send, b_recv = sems[:7]
+    up_send, upa_recv, upb_recv, down_send, down_recv, on_send, two_recv, o_send, o_recv = sems[7:]
+    loads = [pltpu.make_async_copy(ref, raw.at[n], in_sem.at[n]) for n, ref in enumerate((k_ref, v_ref, q_ref))]
+    for load in loads:
+        load.start()
     seq = lax.axis_index("seq")
     y = lax.axis_index("head")
     x = seq // (ZS * CS)
@@ -86,10 +89,17 @@
 
     near = 2 * PEERS
 
+    def by_head(part):
+        loads[part].wait()
+        for group in range(0, PEERS, 16):
+            src_ref[group : group + 16, part * PIECE : (part + 1) * PIECE, :] = pltpu.einshape(
+                "thd->htd", raw[part, :, group : group + 16, :]
+            )
+
+    by_head(0)
+    by_head(1)
     own_kv = pltpu.make_async_copy(src_ref.at[my_head, pl.ds(0, 2 * PIECE)], kv.at[near + my_slot], kv_recv.at[0])
-    own_q = pltpu.make_async_copy(src_ref.at[my_head, pl.ds(2 * PIECE, PIECE)], qs.at[my_slot], q_recv.at[pair])
     own_kv.start()
-    own_q.start()
     pl.semaphore_wait(barrier, PEERS - 1 + 2)
 
     def send_kv(i, carry):
@@ -124,6 +134,9 @@
         return carry
 
     lax.fori_loop(1, WINDOW, send_kv, 0)
+    by_head(2)
+    own_q = pltpu.make_async_copy(src_ref.at[my_head, pl.ds(2 * PIECE, PIECE)], qs.at[my_slot], q_recv.at[pair])
+    own_q.start()
     own_b = pltpu.make_async_copy(own_bias, bias.at[pair], b_recv.at[0])
     own_b.start()
     lax.fori_loop(1, PAIRS, send_bias, 0)
@@ -307,15 +320,15 @@
 
 
 def local(queries, key_vectors, value_vectors, key_blocks):
-    rows = jnp.concatenate([key_vectors, value_vectors, queries], axis=0)
-    by_head = jnp.transpose(rows, (1, 0, 2))
     dma = pltpu.SemaphoreType.DMA
     result = pl.pallas_call(
         kernel,
         out_shape=jax.ShapeDtypeStruct((PEERS, PIECE, 128), jnp.bfloat16),
-        in_specs=[pl.BlockSpec(memory_space=pltpu.SMEM), pl.BlockSpec(memory_space=pltpu.VMEM)],
+        in_specs=[pl.BlockSpec(memory_space=pltpu.SMEM)] + [pl.BlockSpec(memory_space=pltpu.HBM)] * 3,
         out_specs=pl.BlockSpec(memory_space=pltpu.VMEM),
         scratch_shapes=[
+            pltpu.VMEM((3, PIECE, PEERS, 128), jnp.bfloat16),
+            pltpu.VMEM((PEERS, 3 * PIECE, 128), jnp.bfloat16),
             pltpu.VMEM((3 * PEERS, 2 * PIECE, 128), jnp.bfloat16),
             pltpu.VMEM((PEERS, 2 * PIECE, 128), jnp.bfloat16),
             pltpu.VMEM((PEERS, PIECE, 128), jnp.bfloat16),
@@ -323,6 +336,7 @@
             pltpu.VMEM((16, 2 * BLOCK), jnp.float32),
             pltpu.VMEM((PEERS, PIECE, 128), jnp.bfloat16),
             pltpu.VMEM((LEVELS + 1, 2 * BLOCK, 2 * BLOCK), jnp.float32),
+            dma((3,)),
             dma((1,)), dma((PEERS,)),
             dma((1,)), dma((PAIRS,)),
             dma((1,)), dma((1,)),
@@ -332,7 +346,7 @@
             dma((1,)), dma((1,)),
         ],
         compiler_params=pltpu.CompilerParams(collective_id=0, has_side_effects=True, vmem_limit_bytes=48 * 2**20),
-    )(key_blocks, by_head)
+    )(key_blocks, key_vectors, value_vectors, queries)
     return jnp.transpose(result, (1, 0, 2))
 
 

time: 120 us -> 119 us (level)
    unnamed x7 -> x8, local copies, waits for them, and re-layouts: 4.97 us -> 4.35 us
where the time goes in v4:
time: 119 us
  Pallas kernels  113 us (95%)
  local copies, waits for them, and re-layouts  6 us (5%)
    pallas_call x1, Pallas kernels, local(): pl.pallas_call(kernel, out_shape=jax.ShapeDtypeStruct((PEERS, PIECE, 128)...  113 us
    unnamed x8, local copies, waits for them, and re-layouts  4.35 us

profile of v4, /device:TPU:5, one launch (start us, length us, event | category | flops | bytes accessed | tf_op | source)
XLA Modules:
  0.0 119.2 jit_solution(4213489073037847567)
XLA Ops:
  0.0 0.0 copy-start
  0.0 1.2 %copy-done = bf16[64,64,128]{2,1,0:T(8,128)(2,1)S(1)} copy-done((bf16[64,64,128]{2,1,0:T(8,128)(2,1)S(1)}, bf16[64,64,128]{2,1,0:T(8,128)(2,1)}, u32[]{:S(2)}) %copy-start) | copy-done | bytes 1048600
  1.2 0.0 copy-start.1
  1.2 1.2 %copy-done.1 = bf16[64,64,128]{2,1,0:T(8,128)(2,1)S(1)} copy-done((bf16[64,64,128]{2,1,0:T(8,128)(2,1)S(1)}, bf16[64,64,128]{2,1,0:T(8,128)(2,1)}, u32[]{:S(2)}) %copy-start.1) | copy-done | bytes 1048600
  2.5 0.0 copy-start.2
  2.5 1.2 %copy-done.2 = bf16[64,64,128]{2,1,0:T(8,128)(2,1)S(1)} copy-done((bf16[64,64,128]{2,1,0:T(8,128)(2,1)S(1)}, bf16[64,64,128]{2,1,0:T(8,128)(2,1)}, u32[]{:S(2)}) %copy-start.2) | copy-done | bytes 1048600
  3.7 0.0 copy-start.3
  3.7 0.7 copy-done.3
  4.4 113.2 %shard_map.46 = bf16[64,64,128]{2,1,0:T(8,128)(2,1)S(1)} custom-call(s32[2,12]{1,0:T(2,128)S(1)} %copy-done.3, bf16[64,64,128]{2,1,0:T(8,128)(2,1)S(1)} %copy-done, bf16[64,64,128]{2,1,0:T(8,128)(2,1)S(1)} %copy-done.1, bf16[64,64,128]{2,1,0:T(8,128)(2,1)S(1)} %copy-done.2), custom_call_target="tpu_custom_call" | custom-call | tf_op jit(solution)/shard_map/pallas_call | solution.py:324
  117.6 1.6 %copy.5 = bf16[64,64,128]{2,1,0:T(8,128)(2,1)} copy(bf16[64,64,128]{2,0,1:T(8,128)(2,1)S(1)} %bitcast.1) | data formatting | bytes 2097152 | tf_op jit(solution)/shard_map/transpose | solution.py:350
Async XLA Ops:
  0.0 1.2 %copy-start = (bf16[64,64,128]{2,1,0:T(8,128)(2,1)S(1)}, bf16[64,64,128]{2,1,0:T(8,128)(2,1)}, u32[]{:S(2)}) copy-start(bf16[64,64,128]{2,1,0:T(8,128)(2,1)} %k_ref.1) | copy-start | bytes 3145732
  1.2 1.2 %copy-start.1 = (bf16[64,64,128]{2,1,0:T(8,128)(2,1)S(1)}, bf16[64,64,128]{2,1,0:T(8,128)(2,1)}, u32[]{:S(2)}) copy-start(bf16[64,64,128]{2,1,0:T(8,128)(2,1)} %v_ref.1) | copy-start | bytes 3145732
  2.5 1.2 %copy-start.2 = (bf16[64,64,128]{2,1,0:T(8,128)(2,1)S(1)}, bf16[64,64,128]{2,1,0:T(8,128)(2,1)}, u32[]{:S(2)}) copy-start(bf16[64,64,128]{2,1,0:T(8,128)(2,1)} %q_ref.1) | copy-start | bytes 3145732
  3.7 0.7 copy-start.3
